TPU v7x, 512 devices: a whole 4x4x16 slice. The times are simulated.
512 devices in a mesh: au: 16 (over y, x), vert: 32 (over z, core).
Axes of the slice: x: 4, y: 4, z: 16, core: 2. Of those that a mesh axis runs over, the one named last changes fastest.
Arguments:
- visibilities: bfloat16 [12288, 2, 2048], P(('au', 'vert')), may hold values from -6 to 6
- baseline_offsets: float32 [12288, 2, 128], P(('au', 'vert')), may hold values from -8 to 8
- channel_scale: float32 [16], replicated, may hold values from 0.8 to 1.25
- screen_depth: float32 [12288], P(('au', 'vert')), may hold values from -300 to 300
- stations: int32 [12288, 2], P(('au', 'vert')), may hold values from 0 to 511
- corners: int32 [12288, 2], P(('au', 'vert')), may hold values from 0 to 8191, as said below
- beam_terms: bfloat16 [512, 2, 1024], P(('au', 'vert')), may hold values from -5 to 5
Outputs:
- gridded: float32 [8192, 2, 8192], P('au', None, 'vert')
- dirty_image: float32 [8192, 2, 8192], P(('au', 'vert'))
Inputs may be any that keep to these rules, and one draw needn't show every extreme that they name: Subgrid s belongs to block d = floor(s / 24); with d = r * 32 + c, corners[s, 0] lies in [r * 512, (r + 1) * 512) and the columns corners[s, 1] to corners[s, 1] + 31 lie inside one column tile of 256 columns. At most 2 subgrids of one block lie in one column tile; for every r one column tile holds exactly 2 subgrids of every block of that r.
All inputs are finite; a program needn't handle non-finite values.
Results may differ from a plain program's by a relative error of at most 0.039.
Values may be sent and summed in bfloat16 or wider, within the bound.
A program may use at most 64 MiB of HBM per device.

v0:
```python
import math
import jax
import jax.numpy as jnp
from jax import lax
from jax.sharding import PartitionSpec as P

G = 8192
SUB = 32
field_view = 0.1
highest = lax.Precision.HIGHEST


def passed_along(value, axis, steps):
    count = lax.axis_size(axis)
    pairs = [(source, (source + steps) % count) for source in range(count)]
    return lax.ppermute(value, axis, pairs)


def complex_einsum(formula, left_operand_pair, right_pair):
    left_re, left_im = left_operand_pair
    right_re, right_im = right_pair
    real_part = jnp.einsum(formula, left_re, right_re, precision=highest) - jnp.einsum(
        formula, left_im, right_im, precision=highest
    )
    imag_part = jnp.einsum(formula, left_re, right_im, precision=highest) + jnp.einsum(
        formula, left_im, right_re, precision=highest
    )
    return (real_part, imag_part)


def complex_product(left_operand_pair, right_pair):
    return (
        left_operand_pair[0] * right_pair[0] - left_operand_pair[1] * right_pair[1],
        left_operand_pair[0] * right_pair[1] + left_operand_pair[1] * right_pair[0],
    )


def unit_table(row_count, col_count, period):
    product = (
        jnp.arange(row_count, dtype=jnp.int32)[:, None]
        * jnp.arange(col_count, dtype=jnp.int32)[None, :]
        % period
    )
    angle = 2.0 * math.pi / period * product.astype(jnp.float32)
    return (jnp.cos(angle), jnp.sin(angle))


def subgrid_table():
    centred = jnp.arange(SUB, dtype=jnp.int32) - SUB // 2
    product = centred[:, None] * centred[None, :] % SUB
    angle = -2.0 * math.pi / SUB * product.astype(jnp.float32)
    return (jnp.cos(angle) / SUB, jnp.sin(angle) / SUB)


def grid_subgrids(vis_items, offset_items, depth_items, beam_first, beam_second, channel_scale):
    item_count = vis_items.shape[0]
    vis_count = vis_items.shape[2]
    pixel_pos = jnp.arange(SUB, dtype=jnp.float32) - SUB // 2
    shift_u = (offset_items[:, 0, :, None] * channel_scale[None, None, :]).reshape(
        item_count, vis_count
    )
    shift_v = (offset_items[:, 1, :, None] * channel_scale[None, None, :]).reshape(
        item_count, vis_count
    )
    angle_u = 2.0 * math.pi / SUB * pixel_pos[None, :, None] * shift_u[:, None, :]
    angle_v = 2.0 * math.pi / SUB * pixel_pos[None, :, None] * shift_v[:, None, :]
    vis_re = vis_items[:, 0, None, :].astype(jnp.float32)
    vis_im = vis_items[:, 1, None, :].astype(jnp.float32)
    cos_u = jnp.cos(angle_u)
    sin_u = jnp.sin(angle_u)
    weighted_re = (vis_re * cos_u - vis_im * sin_u).astype(jnp.bfloat16)
    weighted_im = (vis_re * sin_u + vis_im * cos_u).astype(jnp.bfloat16)
    phasor_re = jnp.cos(angle_v).astype(jnp.bfloat16)
    phasor_im = jnp.sin(angle_v).astype(jnp.bfloat16)
    stacked_left = jnp.concatenate([weighted_re, weighted_im], axis=2)
    stacked_right = jnp.concatenate(
        [
            jnp.concatenate([phasor_re, -phasor_im], axis=2),
            jnp.concatenate([phasor_im, phasor_re], axis=2),
        ],
        axis=1,
    )
    sky_both = jnp.einsum(
        "npk,nqk->npq", stacked_left, stacked_right, preferred_element_type=jnp.float32
    )
    sky_pair = (sky_both[:, :, :SUB], sky_both[:, :, SUB:])
    taper_line = 1.0 - ((2.0 * jnp.arange(SUB, dtype=jnp.float32) + 1.0 - SUB) / SUB) ** 2
    taper_grid = taper_line[:, None] * taper_line[None, :] / math.sqrt(vis_count)
    sky_angle = pixel_pos * field_view / SUB
    radius_sq = sky_angle[:, None] ** 2 + sky_angle[None, :] ** 2
    screen_angle = -math.pi * depth_items[:, None, None] * radius_sq[None, :, :]
    first_beam = beam_first.astype(jnp.float32).reshape(item_count, 2, SUB, SUB)
    second_beam = beam_second.astype(jnp.float32).reshape(item_count, 2, SUB, SUB)
    pair_term = complex_product(
        (first_beam[:, 0], first_beam[:, 1]), (second_beam[:, 0], -second_beam[:, 1])
    )
    mixed = complex_product(sky_pair, pair_term)
    screened = complex_product(mixed, (jnp.cos(screen_angle), jnp.sin(screen_angle)))
    corrected = (screened[0] * taper_grid, screened[1] * taper_grid)
    dft_pair = subgrid_table()
    partial_pair = complex_einsum("ip,npq->niq", dft_pair, corrected)
    uv_pair = complex_einsum("niq,jq->nij", partial_pair, dft_pair)
    return jnp.stack(uv_pair, axis=1).reshape(item_count, 2 * SUB * SUB)


def grid_in_blocks(vis_items, offset_items, depth_items, first_items, second_items, channel_scale):
    item_count = vis_items.shape[0]
    block_size = math.gcd(item_count, 4)
    block_count = item_count // block_size

    def regroup(source):
        return source.reshape((block_count, block_size) + source.shape[1:])

    def grid_block(pieces):
        return grid_subgrids(
            pieces[0], pieces[1], pieces[2], pieces[3], pieces[4], channel_scale
        ).astype(jnp.bfloat16)

    gridded_blocks = lax.map(
        grid_block,
        (
            regroup(vis_items),
            regroup(offset_items),
            regroup(depth_items),
            regroup(first_items),
            regroup(second_items),
        ),
    )
    return gridded_blocks.reshape(item_count, 2 * SUB * SUB)


def add_subgrids(uv_items, offset_items, tile_rows, tile_cols):
    item_count = uv_items.shape[0]
    pieces = uv_items.reshape(item_count, 2, SUB, SUB)
    span_index = jnp.arange(SUB, dtype=jnp.int32)
    column_index = jnp.arange(tile_cols, dtype=jnp.int32)
    column_onehot = (
        column_index[None, None, :] == offset_items[:, 1, None, None] + span_index[None, :, None]
    ).astype(jnp.bfloat16)
    placed = jnp.einsum("mcij,mjv->micv", pieces, column_onehot, preferred_element_type=jnp.float32)
    row_ids = (offset_items[:, 0, None] + span_index[None, :]).reshape(-1)
    return jax.ops.segment_sum(
        placed.reshape(item_count * SUB, 2 * tile_cols), row_ids, num_segments=tile_rows + SUB
    )


def on_device(
    visibilities, baseline_offsets, channel_scale, screen_depth, stations, corners, beam_terms
):
    au_count = lax.axis_size("au")
    vertical_count = lax.axis_size("vert")
    device_count = au_count * vertical_count
    tile_rows = G // au_count
    tile_cols = G // vertical_count
    own_count = visibilities.shape[0]
    capacity = max(2, (2 * own_count + vertical_count - 1) // vertical_count)
    slot_count = vertical_count * capacity
    beam_table = lax.all_gather(beam_terms, ("au", "vert"), axis=0, tiled=True)
    target = corners[:, 1] // tile_cols
    row_offset = corners[:, 0] - lax.axis_index("au") * tile_rows
    col_offset = corners[:, 1] - target * tile_cols
    offsets = jnp.stack([row_offset, col_offset], axis=1)
    chosen = (target[:, None] == jnp.arange(vertical_count, dtype=jnp.int32)[None, :]).astype(
        jnp.int32
    )
    order_index = jnp.arange(own_count, dtype=jnp.int32)
    earlier_mask = (order_index[None, :] < order_index[:, None]).astype(jnp.int32)
    earlier_count = jnp.dot(earlier_mask, chosen)
    slot_rank = jnp.sum(chosen * earlier_count, axis=1)
    slot_index = target * capacity + slot_rank
    placement = jnp.arange(slot_count, dtype=jnp.int32)[:, None] == slot_index[None, :]
    place_whole = placement.astype(jnp.int32)
    uv_items = grid_in_blocks(
        visibilities,
        baseline_offsets,
        screen_depth,
        jnp.take(beam_table, stations[:, 0], axis=0),
        jnp.take(beam_table, stations[:, 1], axis=0),
        channel_scale,
    )
    uv_send = (
        jnp.dot(placement.astype(jnp.bfloat16), uv_items, preferred_element_type=jnp.float32)
        .astype(jnp.bfloat16)
        .reshape(vertical_count, capacity, -1)
    )
    offset_send = jnp.dot(place_whole, offsets).reshape(vertical_count, capacity, 2)
    uv_slots, offset_slots = (
        lax.all_to_all(uv_send, "vert", split_axis=0, concat_axis=0, tiled=True),
        lax.all_to_all(offset_send, "vert", split_axis=0, concat_axis=0, tiled=True),
    )
    extended = add_subgrids(
        uv_slots.reshape(slot_count, 2 * SUB * SUB),
        offset_slots.reshape(slot_count, 2),
        tile_rows,
        tile_cols,
    )
    carried = passed_along(extended[tile_rows:].astype(jnp.bfloat16), "au", 1).astype(jnp.float32)
    uv_tile = extended[:tile_rows].at[:SUB].add(carried).reshape(tile_rows, 2, tile_cols)
    block_rows = G // device_count
    row_blocks = lax.all_to_all(
        uv_tile.astype(jnp.bfloat16), "vert", split_axis=0, concat_axis=2, tiled=True
    ).astype(uv_tile.dtype)
    split_rows = row_blocks.reshape(block_rows, 2, block_rows, device_count)
    short_table = unit_table(block_rows, block_rows, block_rows)
    long_table = unit_table(device_count, device_count, device_count)
    twist_cols = unit_table(block_rows, device_count, G)
    first_pass = complex_einsum("urj,kr->ukj", (split_rows[:, 0], split_rows[:, 1]), short_table)
    first_pass = complex_product(first_pass, (twist_cols[0][None], twist_cols[1][None]))
    second_pass = complex_einsum("ukj,pj->pku", first_pass, long_table)
    spectra = jnp.stack(second_pass, axis=1).reshape(
        au_count, vertical_count, 2, block_rows * block_rows
    )
    arrived = lax.all_to_all(
        lax.all_to_all(spectra.astype(jnp.bfloat16), "au", split_axis=0, concat_axis=0, tiled=True),
        "vert",
        split_axis=1,
        concat_axis=1,
        tiled=True,
    ).astype(spectra.dtype)
    whole_rows = arrived.reshape(device_count, 2, block_rows, block_rows)
    third_pass = complex_einsum("jkl,qj->qkl", (whole_rows[:, 0], whole_rows[:, 1]), long_table)
    twist_rows = unit_table(device_count, block_rows, G)
    third_pass = complex_product(third_pass, (twist_rows[0][:, None, :], twist_rows[1][:, None, :]))
    fourth_pass = complex_einsum("qkl,pl->kpq", third_pass, short_table)
    image_scale = 1.0 / (SUB * math.sqrt(own_count * device_count))
    dirty_image = jnp.stack(fourth_pass, axis=1).reshape(block_rows, 2, G) * image_scale
    return (uv_tile, dirty_image)


def solution(mesh):
    return jax.shard_map(
        on_device,
        mesh=mesh,
        in_specs=(
            P(("au", "vert"), None, None),
            P(("au", "vert"), None, None),
            P(),
            P(("au", "vert")),
            P(("au", "vert"), None),
            P(("au", "vert"), None),
            P(("au", "vert"), None, None),
        ),
        out_specs=(P("au", None, "vert"), P(("au", "vert"), None, None)),
        check_vma=False,
    )
```

profile of v0, /device:TPU:1, one launch (start us, length us, event | category | flops | bytes accessed | tf_op | source)
XLA Modules:
  0.0 559.0 jit_solution(18145819555831487277)
XLA Ops:
  7.9 0.8 multiply_subtract_fusion.6
  9.0 0.7 multiply_add_fusion.5
  10.6 16.7 %all-to-all-start = ((s32[32,2,2]{1,2,0:T(2,128)}), s32[32,2,2]{1,2,0:T(2,128)S(1)}, u32[]{:S(2)}, u32[]{:S(2)}) async-start(s32[32,2,2]{1,2,0:T(2,128)} %copy.49), calls=%async_computation | async-start | bytes 65536 | tf_op jit(solution)/shard_map/all_to_all | solution.py:189
  27.3 0.7 reshape.464
  28.1 0.8 compare_and_fusion
  28.9 185.3 %all-gather.2.cloned.1.call-done = bf16[512,2,1024]{2,1,0:T(2,128)(2,1)} async-done(((bf16[1,2,1024]{2,1,0:T(2,128)(2,1)}), bf16[512,2,1024]{2,1,0:T(2,128)(2,1)}) %all-gather.2.cloned.1.call-update) | async-done | bytes 2097168 | tf_op jit(solution)/shard_map/all_gather | solution.py:158
  214.1 2.3 gather_fusion
  216.5 2.3 gather_fusion.1
  219.1 119.9 %while.15 = (s32[]{:T(128)}, bf16[6,4,2048]{2,1,0:T(4,128)(2,1)S(1)}, bf16[6,4,2,2048]{3,2,1,0:T(2,128)(2,1)}, f32[6,4,2,128]{3,2,1,0:T(2,128)}, f32[16]{0:T(128...) while((s32[]{:T(128)}, ...), condition=%wide.region_2.4_spmd, body=%wide.region_1.3_spmd.sunk | while | flops 94977376 | bytes 7133457 | solution.py:119
  221.2 0.8 constant_dynamic-slice_fusion.8
  222.0 8.0 %fusion.347 = (bf16[4,32,2048]{2,1,0:T(8,128)(2,1)S(1)}, bf16[4,32,2048]{2,1,0:T(8,128)(2,1)S(1)}, bf16[4,32,2048]{2,1,0:T(8,128)(2,1)S(1)}, bf16[4,32,2048]{2,1,0:T(8,128)(2,1)S(1)}) fusion(f32[4,2048]{1,0:T(4,128)S(1)} %get-tuple-element.319, f32[4,2048]{1,0:T(4,128)S(1)} %get-tuple-element.322, f32[32]{0:T(128)S(1)} %fusion.346, ...), kind=kLoop, calls=%fused_computation.30.clone.1 | loop fusion | flops 3145728 | bytes 2228352 | tf_op jit(solution)/shard_map/while/body/eval_jaxpr/convert_element_type | solution.py:71
  230.0 3.6 fusion.348
  233.6 0.8 fusion.349
  241.1 0.8 constant_dynamic-slice_fusion.8
  242.0 8.0 %fusion.347 = (bf16[4,32,2048]{2,1,0:T(8,128)(2,1)S(1)}, bf16[4,32,2048]{2,1,0:T(8,128)(2,1)S(1)}, bf16[4,32,2048]{2,1,0:T(8,128)(2,1)S(1)}, bf16[4,32,2048]{2,1,0:T(8,128)(2,1)S(1)}) fusion(f32[4,2048]{1,0:T(4,128)S(1)} %get-tuple-element.319, f32[4,2048]{1,0:T(4,128)S(1)} %get-tuple-element.322, f32[32]{0:T(128)S(1)} %fusion.346, ...), kind=kLoop, calls=%fused_computation.30.clone.1 | loop fusion | flops 3145728 | bytes 2228352 | tf_op jit(solution)/shard_map/while/body/eval_jaxpr/convert_element_type | solution.py:71
  250.0 3.6 fusion.348
  253.6 0.8 fusion.349
  261.1 0.8 constant_dynamic-slice_fusion.8
  262.0 8.0 %fusion.347 = (bf16[4,32,2048]{2,1,0:T(8,128)(2,1)S(1)}, bf16[4,32,2048]{2,1,0:T(8,128)(2,1)S(1)}, bf16[4,32,2048]{2,1,0:T(8,128)(2,1)S(1)}, bf16[4,32,2048]{2,1,0:T(8,128)(2,1)S(1)}) fusion(f32[4,2048]{1,0:T(4,128)S(1)} %get-tuple-element.319, f32[4,2048]{1,0:T(4,128)S(1)} %get-tuple-element.322, f32[32]{0:T(128)S(1)} %fusion.346, ...), kind=kLoop, calls=%fused_computation.30.clone.1 | loop fusion | flops 3145728 | bytes 2228352 | tf_op jit(solution)/shard_map/while/body/eval_jaxpr/convert_element_type | solution.py:71
  270.0 3.6 fusion.348
  273.6 0.8 fusion.349
  281.1 0.8 constant_dynamic-slice_fusion.8
  282.0 8.0 %fusion.347 = (bf16[4,32,2048]{2,1,0:T(8,128)(2,1)S(1)}, bf16[4,32,2048]{2,1,0:T(8,128)(2,1)S(1)}, bf16[4,32,2048]{2,1,0:T(8,128)(2,1)S(1)}, bf16[4,32,2048]{2,1,0:T(8,128)(2,1)S(1)}) fusion(f32[4,2048]{1,0:T(4,128)S(1)} %get-tuple-element.319, f32[4,2048]{1,0:T(4,128)S(1)} %get-tuple-element.322, f32[32]{0:T(128)S(1)} %fusion.346, ...), kind=kLoop, calls=%fused_computation.30.clone.1 | loop fusion | flops 3145728 | bytes 2228352 | tf_op jit(solution)/shard_map/while/body/eval_jaxpr/convert_element_type | solution.py:71
  289.9 3.6 fusion.348
  293.5 0.8 fusion.349
  301.1 0.8 constant_dynamic-slice_fusion.8
  301.9 8.0 %fusion.347 = (bf16[4,32,2048]{2,1,0:T(8,128)(2,1)S(1)}, bf16[4,32,2048]{2,1,0:T(8,128)(2,1)S(1)}, bf16[4,32,2048]{2,1,0:T(8,128)(2,1)S(1)}, bf16[4,32,2048]{2,1,0:T(8,128)(2,1)S(1)}) fusion(f32[4,2048]{1,0:T(4,128)S(1)} %get-tuple-element.319, f32[4,2048]{1,0:T(4,128)S(1)} %get-tuple-element.322, f32[32]{0:T(128)S(1)} %fusion.346, ...), kind=kLoop, calls=%fused_computation.30.clone.1 | loop fusion | flops 3145728 | bytes 2228352 | tf_op jit(solution)/shard_map/while/body/eval_jaxpr/convert_element_type | solution.py:71
  309.9 3.6 fusion.348
  313.5 0.8 fusion.349
  321.1 0.8 constant_dynamic-slice_fusion.8
  321.9 8.0 %fusion.347 = (bf16[4,32,2048]{2,1,0:T(8,128)(2,1)S(1)}, bf16[4,32,2048]{2,1,0:T(8,128)(2,1)S(1)}, bf16[4,32,2048]{2,1,0:T(8,128)(2,1)S(1)}, bf16[4,32,2048]{2,1,0:T(8,128)(2,1)S(1)}) fusion(f32[4,2048]{1,0:T(4,128)S(1)} %get-tuple-element.319, f32[4,2048]{1,0:T(4,128)S(1)} %get-tuple-element.322, f32[32]{0:T(128)S(1)} %fusion.346, ...), kind=kLoop, calls=%fused_computation.30.clone.1 | loop fusion | flops 3145728 | bytes 2228352 | tf_op jit(solution)/shard_map/while/body/eval_jaxpr/convert_element_type | solution.py:71
  329.9 3.6 fusion.348
  333.5 0.8 fusion.349
  339.2 0.9 reshape.466
  340.1 7.4 %all-to-all-start.1 = ((bf16[32,2,2048]{2,1,0:T(2,128)(2,1)}), bf16[32,2,2048]{2,1,0:T(2,128)(2,1)S(1)}, u32[]{:S(2)}, u32[]{:S(2)}) async-start(bf16[32,2,2048]{2,1,0:T(2,128)(2,1)} %reshape.466), calls=%async_computation.1 | async-start | bytes 524288 | tf_op jit(solution)/shard_map/all_to_all | solution.py:188
  347.9 21.8 %all-to-all-done.1 = bf16[32,2,2048]{2,1,0:T(2,128)(2,1)S(1)} async-done(((bf16[32,2,2048]{2,1,0:T(2,128)(2,1)}), bf16[32,2,2048]{2,1,0:T(2,128)(2,1)S(1)}, u32[]{:S(2)}, u32[]{:S(2)}) %all-to-all-start.1) | async-done | bytes 262176 | tf_op jit(solution)/shard_map/all_to_all | solution.py:188
  370.2 1.0 convolution_bitcast_fusion
  371.2 3.9 copy.56
  375.1 2.4 copy.81
  377.5 13.5 %scatter_custom_fusion = f32[544,512]{1,0:T(8,128)S(1)} fusion(s32[2048]{0:T(1024)S(1)} %reshape.493, f32[2048,512]{1,0:T(8,128)} %bitcast.254, f32[]{:T(128)} %constant.250.clone.1), kind=kCustom, calls=%fused_computation.192 | custom fusion | flops 1048576 | bytes 1114624 | tf_op jit(solution)/shard_map/scatter-add | solution.py:142
  391.0 3.2 collective-permute-start
  394.2 1.0 slice.178
  395.2 3.7 collective-permute-done
  399.6 1.9 reshape.468
  401.5 1.2 convert_element_type.204
  402.7 5.8 %all-to-all-start.2 = ((bf16[512,2,256]{2,1,0:T(2,128)(2,1)}), bf16[512,2,256]{2,1,0:T(2,128)(2,1)S(1)}, u32[]{:S(2)}, u32[]{:S(2)}) async-start(bf16[512,2,256]{2,1,0:T(2,128)(2,1)} %convert_element_type.204), calls=%async_computation.2 | async-start | bytes 1048576 | tf_op jit(solution)/shard_map/all_to_all | solution.py:200
  408.6 33.0 %all-to-all-done.2 = bf16[512,2,256]{2,1,0:T(2,128)(2,1)S(1)} async-done(((bf16[512,2,256]{2,1,0:T(2,128)(2,1)}), bf16[512,2,256]{2,1,0:T(2,128)(2,1)S(1)}, u32[]{:S(2)}, u32[]{:S(2)}) %all-to-all-start.2) | async-done | bytes 524320 | tf_op jit(solution)/shard_map/all_to_all | solution.py:200
  443.7 5.0 fusion.135
  448.7 5.2 fusion.131
  453.9 5.0 fusion.126
  459.7 0.8 copy.60
  460.5 5.2 fusion.125
  466.5 0.8 copy.61
  467.4 13.5 %all_to_all.35 = bf16[16,32,2,256]{3,1,2,0:T(8,128)(2,1)S(1)} all-to-all(bf16[16,32,2,256]{3,1,2,0:T(8,128)(2,1)S(1)} %pad_maximum_fusion.1), channel_id=1, replica_groups=mesh['au'=16,'vert'=32] {'au'}, dimensions={0} | all-to-all | bytes 1048576 | tf_op jit(solution)/shard_map/all_to_all | solution.py:214
  480.9 1.1 copy.62
  482.0 5.4 all-to-all-start.4
  487.6 33.4 %all-to-all-done.4 = bf16[16,32,2,256]{3,0,2,1:T(8,128)(2,1)S(1)} async-done(((bf16[16,32,2,256]{3,0,2,1:T(8,128)(2,1)}), bf16[16,32,2,256]{3,0,2,1:T(8,128)(2,1)S(1)}, u32[]{:S(2)}, u32[]{:S(2)}) %all-to-all-start.4) | async-done | bytes 524320 | tf_op jit(solution)/shard_map/all_to_all | solution.py:213
  520.9 2.2 copy.63
  523.1 2.1 reshape.470
  525.2 5.0 fusion.150
  530.3 5.1 fusion.158
  535.3 5.1 fusion.156
  540.4 5.3 fusion.152
  549.7 2.1 maximum_multiply_fusion
  (267 shorter events, 51.4 us)
Async XLA Ops:
  7.2 206.9 %all-gather.2.cloned.1.call-start = ((), (), s32[]{:S(2)}) async-start(), calls=%async_computation.5 | async-start | bytes 2101248 | tf_op jit(solution)/shard_map/all_gather | solution.py:158
  10.6 329.5 %all-to-all-start = ((s32[32,2,2]{1,2,0:T(2,128)}), s32[32,2,2]{1,2,0:T(2,128)S(1)}, u32[]{:S(2)}, u32[]{:S(2)}) async-start(s32[32,2,2]{1,2,0:T(2,128)} %copy.49), calls=%async_computation | async-start | bytes 65536 | tf_op jit(solution)/shard_map/all_to_all | solution.py:189
  340.1 29.5 %all-to-all-start.1 = ((bf16[32,2,2048]{2,1,0:T(2,128)(2,1)}), bf16[32,2,2048]{2,1,0:T(2,128)(2,1)S(1)}, u32[]{:S(2)}, u32[]{:S(2)}) async-start(bf16[32,2,2048]{2,1,0:T(2,128)(2,1)} %reshape.466), calls=%async_computation.1 | async-start | bytes 524288 | tf_op jit(solution)/shard_map/all_to_all | solution.py:188
  391.0 8.0 %collective-permute-start = (bf16[32,512]{1,0:T(8,128)(2,1)S(1)}, bf16[32,512]{1,0:T(8,128)(2,1)S(1)}, u32[]{:S(2)}, u32[]{:S(2)}) collective-permute-start(bf16[32,512]{1,0:T(8,128)(2,1)S(1)} %slice.226), channel_id=1, source_target_pairs={{0,32},{32,64},{64,96},{96,128},{128,160},{160,192},{192,224},{224... | collective-permute-start | bytes 98312 | tf_op jit(solution)/shard_map/ppermute | solution.py:16
  401.5 40.5 %copy-start = (f32[512,2,256]{2,1,0:T(2,128)}, f32[512,2,256]{2,1,0:T(2,128)S(1)}, u32[]{:S(2)}) copy-start(f32[512,2,256]{2,1,0:T(2,128)S(1)} %reshape.468) | copy-start | bytes 3145732
  402.7 38.9 %all-to-all-start.2 = ((bf16[512,2,256]{2,1,0:T(2,128)(2,1)}), bf16[512,2,256]{2,1,0:T(2,128)(2,1)S(1)}, u32[]{:S(2)}, u32[]{:S(2)}) async-start(bf16[512,2,256]{2,1,0:T(2,128)(2,1)} %convert_element_type.204), calls=%async_computation.2 | async-start | bytes 1048576 | tf_op jit(solution)/shard_map/all_to_all | solution.py:200
  482.0 39.0 %all-to-all-start.4 = ((bf16[16,32,2,256]{3,0,2,1:T(8,128)(2,1)}), bf16[16,32,2,256]{3,0,2,1:T(8,128)(2,1)S(1)}, u32[]{:S(2)}, u32[]{:S(2)}) async-start(bf16[16,32,2,256]{3,0,2,1:T(8,128)(2,1)} %copy.62), calls=%async_computation.4 | async-start | bytes 1048576 | tf_op jit(solution)/shard_map/all_to_all | solution.py:213
Sparse Core Ops, SparseCore 0:
  12.6 201.5 all-gather.1
where the time goes:
time: 568 us; the launch traced here: 559 us
  waiting for transfers between devices  278 us (49%)
  other arithmetic  92.1 us (16%)
  matrix products  74.3 us (13%)
  local copies, waits for them, and re-layouts  46.4 us (8%)
  starting transfers between devices  38.5 us (7%)
  between operations  14.9 us (3%)
  blocking collectives  13.5 us (2%)
    all_gather x1, waiting for transfers between devices, on_device(): beam_table = lax.all_gather(beam_terms, ('au', 'vert'), axis=0, tiled=True)  185 us
    convert_element_type x6, other arithmetic, grid_subgrids(): weighted_re = (vis_re * cos_u - vis_im * sin_u).astype(jnp.bfloat16)  47.8 us
    all_to_all x1, waiting for transfers between devices, on_device(): lax.all_to_all(lax.all_to_all(spectra.astype(jnp.bfloat16), 'au', split_a...  33.4 us
    all_to_all x1, waiting for transfers between devices, on_device(): lax.all_to_all(uv_tile.astype(jnp.bfloat16), 'vert', split_axis=0, concat...  33 us
    all_to_all x1, waiting for transfers between devices, on_device(): lax.all_to_all(uv_send, 'vert', split_axis=0, concat_axis=0, tiled=True)  21.8 us
    neg x6, other arithmetic, grid_subgrids(): -phasor_im  21.6 us
    unnamed x4, matrix products  20.4 us
    all_to_all x1, starting transfers between devices, on_device(): lax.all_to_all(offset_send, 'vert', split_axis=0, concat_axis=0, tiled=True)  16.7 us
  transfers between devices with their start and end apart: 6, of which 5 were waited for; matrix products, arithmetic and copies ran while one was open for 23% of the time, Pallas kernels for 0%

commit v1 on v0

--- a/solution.py
+++ b/solution.py
@@ -155,7 +155,8 @@
     own_count = visibilities.shape[0]
     capacity = max(2, (2 * own_count + vertical_count - 1) // vertical_count)
     slot_count = vertical_count * capacity
-    beam_table = lax.all_gather(beam_terms, ("au", "vert"), axis=0, tiled=True)
+    stack = jnp.stack([beam_terms] * lax.axis_size(("au", "vert")))
+    beam_table = jnp.concatenate(lax.all_to_all(stack, ("au", "vert"), 0, 0), axis=0)
     target = corners[:, 1] // tile_cols
     row_offset = corners[:, 0] - lax.axis_index("au") * tile_rows
     col_offset = corners[:, 1] - target * tile_cols

time: 568 us -> 476 us (0.84)
  waiting for transfers between devices: 278 us -> 192 us
  starting transfers between devices: 38.5 us -> 57 us
  between operations: 14.9 us -> 1.31 us
    all_gather x1 -> x0, waiting for transfers between devices: 185 us -> none  [on_device(): beam_table = lax.all_gather(beam_terms, ('au', 'vert'), axis=0, tiled=True)]
    all_to_all x0 -> x1, waiting for transfers between devices: none -> 99.4 us  [on_device(): lax.all_to_all(stack, ('au', 'vert'), 0, 0)]
    all_to_all x0 -> x1, starting transfers between devices: none -> 24.3 us  [on_device(): lax.all_to_all(stack, ('au', 'vert'), 0, 0)]
    all_to_all x1, starting transfers between devices: 16.7 us -> 6.21 us  [on_device(): lax.all_to_all(offset_send, 'vert', split_axis=0, concat_axis=0, tiled=True)]
  transfers between devices with their start and end apart: 6 -> 6, of which waited for: 5 -> 5; matrix products, arithmetic and copies ran while one was open for 23% -> 26% of each run, Pallas kernels for 0% -> 0%
where the time goes in v1:
time: 476 us; the launch traced here: 471 us
  waiting for transfers between devices  192 us (40%)
  other arithmetic  90 us (19%)
  matrix products  74.5 us (16%)
  starting transfers between devices  57 us (12%)
  local copies, waits for them, and re-layouts  41.8 us (9%)
  blocking collectives  13.2 us (3%)
    all_to_all x1, waiting for transfers between devices, on_device(): lax.all_to_all(stack, ('au', 'vert'), 0, 0)  99.4 us
    convert_element_type x6, other arithmetic, grid_subgrids(): weighted_re = (vis_re * cos_u - vis_im * sin_u).astype(jnp.bfloat16)  47.8 us
    all_to_all x1, waiting for transfers between devices, on_device(): lax.all_to_all(lax.all_to_all(spectra.astype(jnp.bfloat16), 'au', split_a...  33.4 us
    all_to_all x1, waiting for transfers between devices, on_device(): lax.all_to_all(uv_tile.astype(jnp.bfloat16), 'vert', split_axis=0, concat...  33.2 us
    all_to_all x1, starting transfers between devices, on_device(): lax.all_to_all(stack, ('au', 'vert'), 0, 0)  24.3 us
    all_to_all x1, waiting for transfers between devices, on_device(): lax.all_to_all(uv_send, 'vert', split_axis=0, concat_axis=0, tiled=True)  21.8 us
    neg x6, other arithmetic, grid_subgrids(): -phasor_im  21.6 us
    unnamed x4, matrix products  20.4 us
  transfers between devices with their start and end apart: 6, of which 5 were waited for; matrix products, arithmetic and copies ran while one was open for 26% of the time, Pallas kernels for 0%

profile of v1, /device:TPU:1, one launch (start us, length us, event | category | flops | bytes accessed | tf_op | source)
XLA Modules:
  0.0 470.9 jit_solution(4168018297234436505)
XLA Ops:
  0.6 3.1 stack.44
  3.7 24.3 %all-to-all-start.1 = ((bf16[512,1,2,1024]{3,2,1,0:T(2,128)(2,1)}), bf16[512,1,2,1024]{3,2,1,0:T(2,128)(2,1)S(1)}, u32[]{:S(2)}, u32[]{:S(2)}) async-start(bf16[512,1,2,1024]{3,2,1,0:T(2,128)(2,1)} %stack.44), calls=%async_computation.1 | async-start | bytes 4194304 | tf_op jit(solution)/shard_map/all_to_all | solution.py:159
  29.4 99.4 %all-to-all-done.1 = bf16[512,1,2,1024]{3,2,1,0:T(2,128)(2,1)S(1)} async-done(((bf16[512,1,2,1024]{3,2,1,0:T(2,128)(2,1)}), bf16[512,1,2,1024]{3,2,1,0:T(2,128)(2,1)S(1)}, u32[]{:S(2)}, u32[]{:S(2)}) %all-to-all-start.1) | async-done | bytes 2097184 | tf_op jit(solution)/shard_map/all_to_all | solution.py:159
  128.9 6.2 %all-to-all-start = ((s32[32,2,2]{1,2,0:T(2,128)}), s32[32,2,2]{1,2,0:T(2,128)S(1)}, u32[]{:S(2)}, u32[]{:S(2)}) async-start(s32[32,2,2]{1,2,0:T(2,128)} %copy.49), calls=%async_computation | async-start | bytes 65536 | tf_op jit(solution)/shard_map/all_to_all | solution.py:190
  135.1 0.8 gather_fusion
  135.8 0.8 gather_fusion.1
  136.9 116.0 %while.15 = (s32[]{:T(128)}, bf16[6,4,2048]{2,1,0:T(4,128)(2,1)S(1)}, bf16[6,4,2,2048]{3,2,1,0:T(2,128)(2,1)}, f32[6,4,2,128]{3,2,1,0:T(2,128)}, f32[16]{0:T(128...) while((s32[]{:T(128)}, ...), condition=%wide.region_2.4_spmd, body=%wide.region_1.3_spmd.sunk | while | flops 94977376 | bytes 7133457 | solution.py:119
  136.9 0.7 constant_dynamic-slice_fusion.9
  138.3 0.8 constant_dynamic-slice_fusion.8
  139.2 8.0 %fusion.347 = (bf16[4,32,2048]{2,1,0:T(8,128)(2,1)S(1)}, bf16[4,32,2048]{2,1,0:T(8,128)(2,1)S(1)}, bf16[4,32,2048]{2,1,0:T(8,128)(2,1)S(1)}, bf16[4,32,2048]{2,1,0:T(8,128)(2,1)S(1)}) fusion(f32[4,2048]{1,0:T(4,128)S(1)} %get-tuple-element.319, f32[4,2048]{1,0:T(4,128)S(1)} %get-tuple-element.322, f32[32]{0:T(128)S(1)} %fusion.346, ...), kind=kLoop, calls=%fused_computation.30.clone.1 | loop fusion | flops 3145728 | bytes 2228352 | tf_op jit(solution)/shard_map/while/body/eval_jaxpr/convert_element_type | solution.py:71
  147.1 3.6 fusion.348
  150.7 0.8 fusion.349
  156.2 0.7 constant_dynamic-slice_fusion.9
  157.6 0.8 constant_dynamic-slice_fusion.8
  158.5 8.0 %fusion.347 = (bf16[4,32,2048]{2,1,0:T(8,128)(2,1)S(1)}, bf16[4,32,2048]{2,1,0:T(8,128)(2,1)S(1)}, bf16[4,32,2048]{2,1,0:T(8,128)(2,1)S(1)}, bf16[4,32,2048]{2,1,0:T(8,128)(2,1)S(1)}) fusion(f32[4,2048]{1,0:T(4,128)S(1)} %get-tuple-element.319, f32[4,2048]{1,0:T(4,128)S(1)} %get-tuple-element.322, f32[32]{0:T(128)S(1)} %fusion.346, ...), kind=kLoop, calls=%fused_computation.30.clone.1 | loop fusion | flops 3145728 | bytes 2228352 | tf_op jit(solution)/shard_map/while/body/eval_jaxpr/convert_element_type | solution.py:71
  166.5 3.6 fusion.348
  170.1 0.8 fusion.349
  177.0 0.8 constant_dynamic-slice_fusion.8
  177.8 8.0 %fusion.347 = (bf16[4,32,2048]{2,1,0:T(8,128)(2,1)S(1)}, bf16[4,32,2048]{2,1,0:T(8,128)(2,1)S(1)}, bf16[4,32,2048]{2,1,0:T(8,128)(2,1)S(1)}, bf16[4,32,2048]{2,1,0:T(8,128)(2,1)S(1)}) fusion(f32[4,2048]{1,0:T(4,128)S(1)} %get-tuple-element.319, f32[4,2048]{1,0:T(4,128)S(1)} %get-tuple-element.322, f32[32]{0:T(128)S(1)} %fusion.346, ...), kind=kLoop, calls=%fused_computation.30.clone.1 | loop fusion | flops 3145728 | bytes 2228352 | tf_op jit(solution)/shard_map/while/body/eval_jaxpr/convert_element_type | solution.py:71
  185.8 3.6 fusion.348
  189.4 0.8 fusion.349
  196.3 0.8 constant_dynamic-slice_fusion.8
  197.2 8.0 %fusion.347 = (bf16[4,32,2048]{2,1,0:T(8,128)(2,1)S(1)}, bf16[4,32,2048]{2,1,0:T(8,128)(2,1)S(1)}, bf16[4,32,2048]{2,1,0:T(8,128)(2,1)S(1)}, bf16[4,32,2048]{2,1,0:T(8,128)(2,1)S(1)}) fusion(f32[4,2048]{1,0:T(4,128)S(1)} %get-tuple-element.319, f32[4,2048]{1,0:T(4,128)S(1)} %get-tuple-element.322, f32[32]{0:T(128)S(1)} %fusion.346, ...), kind=kLoop, calls=%fused_computation.30.clone.1 | loop fusion | flops 3145728 | bytes 2228352 | tf_op jit(solution)/shard_map/while/body/eval_jaxpr/convert_element_type | solution.py:71
  205.1 3.6 fusion.348
  208.7 0.8 fusion.349
  215.6 0.8 constant_dynamic-slice_fusion.8
  216.5 8.0 %fusion.347 = (bf16[4,32,2048]{2,1,0:T(8,128)(2,1)S(1)}, bf16[4,32,2048]{2,1,0:T(8,128)(2,1)S(1)}, bf16[4,32,2048]{2,1,0:T(8,128)(2,1)S(1)}, bf16[4,32,2048]{2,1,0:T(8,128)(2,1)S(1)}) fusion(f32[4,2048]{1,0:T(4,128)S(1)} %get-tuple-element.319, f32[4,2048]{1,0:T(4,128)S(1)} %get-tuple-element.322, f32[32]{0:T(128)S(1)} %fusion.346, ...), kind=kLoop, calls=%fused_computation.30.clone.1 | loop fusion | flops 3145728 | bytes 2228352 | tf_op jit(solution)/shard_map/while/body/eval_jaxpr/convert_element_type | solution.py:71
  224.5 3.6 fusion.348
  228.1 0.8 fusion.349
  235.0 0.8 constant_dynamic-slice_fusion.8
  235.8 8.0 %fusion.347 = (bf16[4,32,2048]{2,1,0:T(8,128)(2,1)S(1)}, bf16[4,32,2048]{2,1,0:T(8,128)(2,1)S(1)}, bf16[4,32,2048]{2,1,0:T(8,128)(2,1)S(1)}, bf16[4,32,2048]{2,1,0:T(8,128)(2,1)S(1)}) fusion(f32[4,2048]{1,0:T(4,128)S(1)} %get-tuple-element.319, f32[4,2048]{1,0:T(4,128)S(1)} %get-tuple-element.322, f32[32]{0:T(128)S(1)} %fusion.346, ...), kind=kLoop, calls=%fused_computation.30.clone.1 | loop fusion | flops 3145728 | bytes 2228352 | tf_op jit(solution)/shard_map/while/body/eval_jaxpr/convert_element_type | solution.py:71
  243.8 3.6 fusion.348
  247.4 0.8 fusion.349
  253.1 0.9 reshape.473
  254.0 12.6 %all-to-all-start.2 = ((bf16[32,2,2048]{2,1,0:T(2,128)(2,1)}), bf16[32,2,2048]{2,1,0:T(2,128)(2,1)S(1)}, u32[]{:S(2)}, u32[]{:S(2)}) async-start(bf16[32,2,2048]{2,1,0:T(2,128)(2,1)} %reshape.473), calls=%async_computation.2 | async-start | bytes 524288 | tf_op jit(solution)/shard_map/all_to_all | solution.py:189
  267.0 21.8 %all-to-all-done.2 = bf16[32,2,2048]{2,1,0:T(2,128)(2,1)S(1)} async-done(((bf16[32,2,2048]{2,1,0:T(2,128)(2,1)}), bf16[32,2,2048]{2,1,0:T(2,128)(2,1)S(1)}, u32[]{:S(2)}, u32[]{:S(2)}) %all-to-all-start.2) | async-done | bytes 262176 | tf_op jit(solution)/shard_map/all_to_all | solution.py:189
  289.2 1.0 convolution_bitcast_fusion
  290.3 3.9 copy.56
  294.2 2.4 copy.81
  296.6 13.5 %scatter_custom_fusion = f32[544,512]{1,0:T(8,128)S(1)} fusion(s32[2048]{0:T(1024)S(1)} %reshape.500, f32[2048,512]{1,0:T(8,128)} %bitcast.256, f32[]{:T(128)} %constant.250.clone.1), kind=kCustom, calls=%fused_computation.192 | custom fusion | flops 1048576 | bytes 1114624 | tf_op jit(solution)/shard_map/scatter-add | solution.py:142
  310.1 2.9 collective-permute-start
  313.0 1.0 slice.178
  314.0 4.0 collective-permute-done
  318.7 1.9 reshape.475
  320.6 1.2 convert_element_type.204
  321.8 5.6 %all-to-all-start.3 = ((bf16[512,2,256]{2,1,0:T(2,128)(2,1)}), bf16[512,2,256]{2,1,0:T(2,128)(2,1)S(1)}, u32[]{:S(2)}, u32[]{:S(2)}) async-start(bf16[512,2,256]{2,1,0:T(2,128)(2,1)} %convert_element_type.204), calls=%async_computation.3 | async-start | bytes 1048576 | tf_op jit(solution)/shard_map/all_to_all | solution.py:201
  327.5 33.2 %all-to-all-done.3 = bf16[512,2,256]{2,1,0:T(2,128)(2,1)S(1)} async-done(((bf16[512,2,256]{2,1,0:T(2,128)(2,1)}), bf16[512,2,256]{2,1,0:T(2,128)(2,1)S(1)}, u32[]{:S(2)}, u32[]{:S(2)}) %all-to-all-start.3) | async-done | bytes 524320 | tf_op jit(solution)/shard_map/all_to_all | solution.py:201
  362.8 5.0 %fusion.135 = f32[512,16,16]{0,2,1:T(8,128)S(1)} fusion(f32[16,16,512]{2,0,1:T(8,128)S(1)} %convolution_add_fusion.3, f32[16,16,512]{2,0,1:T(8,128)S(1)} %convolution_subtract_fusion.3, f32[16,512]{1,0:T(8,128)S(1)} %get-tuple-element.249, f32[16,512]{1,0:T(8,128)S(1)} %get-tuple-element.250), kind=kOutput, calls=%fused_computation.186 | convolution fusion | flops 809369600 | bytes 1638400 | tf_op jit(solution)/shard_map/ukj,pj->pku/dot_general | solution.py:22
  367.8 5.5 %fusion.131 = f32[512,16,16]{0,2,1:T(8,128)S(1)} fusion(f32[16,16,512]{2,0,1:T(8,128)S(1)} %convolution_add_fusion.3, f32[16,16,512]{2,0,1:T(8,128)S(1)} %convolution_subtract_fusion.3, f32[16,512]{1,0:T(8,128)S(1)} %get-tuple-element.249, f32[16,512]{1,0:T(8,128)S(1)} %get-tuple-element.250), kind=kOutput, calls=%fused_computation.182 | convolution fusion | flops 809369600 | bytes 1638400 | tf_op jit(solution)/shard_map/ukj,pj->pku/dot_general | solution.py:25
  373.3 5.0 %fusion.126 = bf16[512,16,16]{0,1,2:T(8,128)(2,1)S(1)} fusion(f32[512,16,16]{0,2,1:T(8,128)S(1)} %fusion.135, f32[16,16,512]{2,0,1:T(8,128)S(1)} %convolution_add_fusion.3, f32[16,16,512]{2,0,1:T(8,128)S(1)} %convolution_subtract_fusion.3, f32[16,512]{1,0:T(8,128)S(1)} %get-tuple-element.249, f32[16,512]{1,0:T(8,128)S(1)} %get-tuple-element.250), kind=kOutput, calls=%fused_computation.175 | convolution fusion | flops 809631744 | bytes 1900544 | tf_op jit(solution)/shard_map/ukj,pj->pku/dot_general | solution.py:22
  379.0 0.8 copy.60
  379.9 5.2 %fusion.125 = bf16[512,16,16]{0,1,2:T(8,128)(2,1)S(1)} fusion(f32[512,16,16]{0,2,1:T(8,128)S(1)} %fusion.131, f32[16,16,512]{2,0,1:T(8,128)S(1)} %convolution_add_fusion.3, f32[16,16,512]{2,0,1:T(8,128)S(1)} %convolution_subtract_fusion.3, f32[16,512]{1,0:T(8,128)S(1)} %get-tuple-element.249, f32[16,512]{1,0:T(8,128)S(1)} %get-tuple-element.250), kind=kOutput, calls=%fused_computation.174 | convolution fusion | flops 809631744 | bytes 1900544 | tf_op jit(solution)/shard_map/ukj,pj->pku/dot_general | solution.py:25
  385.8 0.8 copy.61
  386.7 13.2 %all_to_all.40 = bf16[16,32,2,256]{3,1,2,0:T(8,128)(2,1)S(1)} all-to-all(bf16[16,32,2,256]{3,1,2,0:T(8,128)(2,1)S(1)} %pad_maximum_fusion.1), channel_id=1, replica_groups=mesh['au'=16,'vert'=32] {'au'}, dimensions={0} | all-to-all | bytes 1048576 | tf_op jit(solution)/shard_map/all_to_all | solution.py:215
  399.9 1.1 copy.62
  401.0 5.4 %all-to-all-start.5 = ((bf16[16,32,2,256]{3,0,2,1:T(8,128)(2,1)}), bf16[16,32,2,256]{3,0,2,1:T(8,128)(2,1)S(1)}, u32[]{:S(2)}, u32[]{:S(2)}) async-start(bf16[16,32,2,256]{3,0,2,1:T(8,128)(2,1)} %copy.62), calls=%async_computation.5 | async-start | bytes 1048576 | tf_op jit(solution)/shard_map/all_to_all | solution.py:214
  406.6 33.4 %all-to-all-done.5 = bf16[16,32,2,256]{3,0,2,1:T(8,128)(2,1)S(1)} async-done(((bf16[16,32,2,256]{3,0,2,1:T(8,128)(2,1)}), bf16[16,32,2,256]{3,0,2,1:T(8,128)(2,1)S(1)}, u32[]{:S(2)}, u32[]{:S(2)}) %all-to-all-start.5) | async-done | bytes 524320 | tf_op jit(solution)/shard_map/all_to_all | solution.py:214
  439.9 2.2 copy.63
  442.1 2.1 reshape.477
  444.2 5.0 %fusion.150 = f32[512,256]{0,1:S(1)} fusion(bf16[512,256]{0,1:T(8,128)(2,1)S(1)} %bitcast.271), kind=kOutput, calls=%fused_computation.206 | convolution fusion | flops 808976384 | bytes 786432
  449.3 5.1 %fusion.158 = f32[512,256]{0,1:S(1)} fusion(bf16[512,256]{0,1:T(8,128)(2,1)S(1)} %bitcast.272), kind=kOutput, calls=%fused_computation.209 | convolution fusion | flops 808976384 | bytes 786432
  454.3 5.1 %fusion.156 = f32[512,256]{0,1:S(1)} fusion(bf16[512,256]{0,1:T(8,128)(2,1)S(1)} %bitcast.269), kind=kOutput, calls=%fused_computation.208 | convolution fusion | flops 808976384 | bytes 786432
  459.4 5.2 %fusion.152 = f32[512,256]{0,1:S(1)} fusion(bf16[512,256]{0,1:T(8,128)(2,1)S(1)} %bitcast.270), kind=kOutput, calls=%fused_computation.207 | convolution fusion | flops 808976384 | bytes 786432
  468.7 2.1 maximum_multiply_fusion
  (275 shorter events, 45.5 us)
Async XLA Ops:
  3.7 24.3 %copy-start.4 = (f32[24]{0:T(128)S(1)}, f32[24]{0:T(128)}, u32[]{:S(2)}) copy-start(f32[24]{0:T(128)} %param.16) | copy-start | bytes 292
  3.7 24.4 %copy-start.2 = (s32[24,2]{0,1:T(2,128)S(1)}, s32[24,2]{0,1:T(2,128)}, u32[]{:S(2)}) copy-start(s32[24,2]{0,1:T(2,128)} %param.18) | copy-start | bytes 580
  3.7 25.7 %copy-start.3 = (s32[24,2]{0,1:T(2,128)S(1)}, s32[24,2]{0,1:T(2,128)}, u32[]{:S(2)}) copy-start(s32[24,2]{0,1:T(2,128)} %param.17) | copy-start | bytes 580
  3.7 133.1 %copy-start.1 = (f32[16]{0:T(128)S(1)}, f32[16]{0:T(128)}, u32[]{:S(2)}) copy-start(f32[16]{0:T(128)} %param.15) | copy-start | bytes 196
  3.7 125.1 %all-to-all-start.1 = ((bf16[512,1,2,1024]{3,2,1,0:T(2,128)(2,1)}), bf16[512,1,2,1024]{3,2,1,0:T(2,128)(2,1)S(1)}, u32[]{:S(2)}, u32[]{:S(2)}) async-start(bf16[512,1,2,1024]{3,2,1,0:T(2,128)(2,1)} %stack.44), calls=%async_computation.1 | async-start | bytes 4194304 | tf_op jit(solution)/shard_map/all_to_all | solution.py:159
  128.9 125.2 %all-to-all-start = ((s32[32,2,2]{1,2,0:T(2,128)}), s32[32,2,2]{1,2,0:T(2,128)S(1)}, u32[]{:S(2)}, u32[]{:S(2)}) async-start(s32[32,2,2]{1,2,0:T(2,128)} %copy.49), calls=%async_computation | async-start | bytes 65536 | tf_op jit(solution)/shard_map/all_to_all | solution.py:190
  254.0 34.7 %all-to-all-start.2 = ((bf16[32,2,2048]{2,1,0:T(2,128)(2,1)}), bf16[32,2,2048]{2,1,0:T(2,128)(2,1)S(1)}, u32[]{:S(2)}, u32[]{:S(2)}) async-start(bf16[32,2,2048]{2,1,0:T(2,128)(2,1)} %reshape.473), calls=%async_computation.2 | async-start | bytes 524288 | tf_op jit(solution)/shard_map/all_to_all | solution.py:189
  310.1 8.0 %collective-permute-start = (bf16[32,512]{1,0:T(8,128)(2,1)S(1)}, bf16[32,512]{1,0:T(8,128)(2,1)S(1)}, u32[]{:S(2)}, u32[]{:S(2)}) collective-permute-start(bf16[32,512]{1,0:T(8,128)(2,1)S(1)} %slice.226), channel_id=1, source_target_pairs={{0,32},{32,64},{64,96},{96,128},{128,160},{160,192},{192,224},{224... | collective-permute-start | bytes 98312 | tf_op jit(solution)/shard_map/ppermute | solution.py:16
  320.6 40.5 %copy-start = (f32[512,2,256]{2,1,0:T(2,128)}, f32[512,2,256]{2,1,0:T(2,128)S(1)}, u32[]{:S(2)}) copy-start(f32[512,2,256]{2,1,0:T(2,128)S(1)} %reshape.475) | copy-start | bytes 3145732
  321.8 38.9 %all-to-all-start.3 = ((bf16[512,2,256]{2,1,0:T(2,128)(2,1)}), bf16[512,2,256]{2,1,0:T(2,128)(2,1)S(1)}, u32[]{:S(2)}, u32[]{:S(2)}) async-start(bf16[512,2,256]{2,1,0:T(2,128)(2,1)} %convert_element_type.204), calls=%async_computation.3 | async-start | bytes 1048576 | tf_op jit(solution)/shard_map/all_to_all | solution.py:201
  401.0 39.0 %all-to-all-start.5 = ((bf16[16,32,2,256]{3,0,2,1:T(8,128)(2,1)}), bf16[16,32,2,256]{3,0,2,1:T(8,128)(2,1)S(1)}, u32[]{:S(2)}, u32[]{:S(2)}) async-start(bf16[16,32,2,256]{3,0,2,1:T(8,128)(2,1)} %copy.62), calls=%async_computation.5 | async-start | bytes 1048576 | tf_op jit(solution)/shard_map/all_to_all | solution.py:214
